TPU v7x, 32 devices: a whole 2x2x4 slice. The times are simulated.
32 devices in a mesh: grp: 2 (over x), lon: 8 (over z, y), lat: 2 (over core).
Axes of the slice: x: 2, y: 2, z: 4, core: 2. Of those that a mesh axis runs over, the one named last changes fastest.
Arguments:
- cloud_state: float32 [4, 256, 128, 1024], P('grp', 'lon', 'lat'), parts along dimension 0, may hold values from -6 to 6
- counts: int32 [512, 128], P(('grp', 'lon'), 'lat'), parts along dimension 0, may hold values from 1 to 8, as said below
- courant: float32 [32], replicated, may hold values from 0.2 to 0.9
- truncation: int32 [96], replicated, may hold values from 0 to 94, as said below
Outputs:
- cloud_next: float32 [4, 256, 128, 1024], P('grp', 'lon', 'lat'), parts along dimension 0
There are 2 independent parts, one for each index of `grp`. A program takes and returns all parts, laid end to end along the dimension named above; an argument that names none is the same for every part. Nothing has to cross between parts.
Inputs may be any that keep to these rules, and one draw needn't show every extreme that they name: `counts`: columns come in busy regions of 4 to 8 substeps and calm ones of 1 or 2; column 0, 0 has 8. truncation[m] lies in m .. 85 for m <= 85, truncation[0] = 85, and truncation[m] = m - 1 (nothing kept) for m > 85.
All inputs are finite; a program needn't handle non-finite values.
Results may differ from a plain program's by a relative error of at most 0.0003.
Values sent between devices are 32-bit elements; how exact they have to be, the bound alone decides.
No kernel may reach another device: no remote copies, remote signals or barrier semaphores. Data moves between devices by JAX's collectives and lax.ppermute only.
A program may use at most 64 MiB of HBM per device.

v0:
```python
import jax
import jax.numpy as jnp
from jax import lax
from jax.sharding import PartitionSpec as P

NN = 96
couple_gain = 8.0


def legendre(orders, lat_rows, lat_total, degrees):
    latitude = -0.5 * jnp.pi + jnp.pi * (lat_rows.astype(jnp.float32) + 0.5) / lat_total
    sin_lat = jnp.sin(latitude)
    cos_lat = jnp.cos(latitude)
    order_f = orders.astype(jnp.float32)
    ladder = jnp.arange(1, degrees + 1).astype(jnp.float32)
    log_gains = 0.5 * jnp.log((2.0 * ladder + 1.0) / (2.0 * ladder))
    included = (ladder[None, :] <= order_f[:, None]).astype(jnp.float32)
    log_start = 0.5 * jnp.log(jnp.float32(0.5)) + jnp.sum(included * log_gains[None, :], axis=1)
    diagonal = jnp.exp(log_start[:, None] + order_f[:, None] * jnp.log(cos_lat)[None, :])

    def legendre_advance(carry, degree):
        previous, earlier, inverse = carry
        degree_f = degree.astype(jnp.float32)
        higher = degree_f > order_f
        numerator = jnp.maximum(4.0 * degree_f * degree_f - 1.0, 1.0)
        denominator = jnp.where(higher, degree_f * degree_f - order_f * order_f, 1.0)
        factor = jnp.sqrt(numerator / denominator)
        raised = factor[:, None] * (sin_lat[None, :] * previous - inverse[:, None] * earlier)
        current = jnp.where(
            (degree_f == order_f)[:, None], diagonal, jnp.where(higher[:, None], raised, 0.0)
        )
        return ((current, previous, jnp.where(higher, 1.0 / factor, 0.0)), current)

    initial = (jnp.zeros_like(diagonal), jnp.zeros_like(diagonal), jnp.zeros_like(order_f))
    _, stacked = lax.scan(legendre_advance, initial, jnp.arange(degrees, dtype=jnp.int32), unroll=8)
    return jnp.transpose(stacked, (1, 0, 2))


def latitude_weights(lat_rows, lat_total):
    latitude = -0.5 * jnp.pi + jnp.pi * (lat_rows.astype(jnp.float32) + 0.5) / lat_total
    return jnp.pi * jnp.cos(latitude) / lat_total


def wave_table(lon_rows, modes, lon_total):
    phase = lon_rows[:, None] * modes[None, :] % lon_total
    angle = phase.astype(jnp.float32) * (2.0 * jnp.pi / lon_total)
    return (jnp.cos(angle), jnp.sin(angle))


def substep(theta, moist, force, count, index, rate, profile, levels):
    heated = theta + couple_gain * profile[None, None, :] * force[:, :, None]
    moved_theta = heated - rate * (heated - jnp.roll(heated, levels, axis=2))
    moved_moist = moist - rate * (moist - jnp.roll(moist, levels, axis=2))
    excess = moved_moist - (1.0 + 0.2 * moved_theta)
    condensed = 0.25 * (excess + jnp.sqrt(excess * excess + 0.01))
    active = (index < count)[:, :, None]
    return (
        jnp.where(active, moved_theta + 0.5 * condensed, theta),
        jnp.where(active, moved_moist - condensed, moist),
    )


def run_block(block_state, force_rows, count_rows, rate, profile, levels, trip_count):

    def unfinished(carry):
        return carry[0] < trip_count

    def run_advance(carry):
        index, theta, moist = carry
        theta, moist = substep(theta, moist, force_rows, count_rows, index, rate, profile, levels)
        return (index + 1, theta, moist)

    _, theta, moist = lax.while_loop(
        unfinished, run_advance, (jnp.int32(0), block_state[0], block_state[1])
    )
    return jnp.stack([theta, moist])


def shards(cloud_state, counts, courant, truncation):
    highest = lax.Precision.HIGHEST
    lon_devices = lax.axis_size("lon")
    lon_index = lax.axis_index("lon")
    lat_index = lax.axis_index("lat")
    fields, lon_local, lat_local, cells = cloud_state.shape
    levels = courant.shape[0]
    columns_across = cells // levels
    total_lon = lon_local * lon_devices
    total_lat = lat_local * lax.axis_size("lat")
    total_modes = truncation.shape[0]
    mode_local = total_modes // lon_devices
    heating = jnp.mean(cloud_state[0], axis=2)
    my_lons = lon_index * lon_local + jnp.arange(lon_local, dtype=jnp.int32)
    modes = jnp.arange(mode_local * lax.axis_size("lon"), dtype=jnp.int32)
    cosine_table, sine_table = wave_table(my_lons, modes, total_lon)
    coefs = lax.psum_scatter(
        jnp.stack(
            [
                jnp.dot(cosine_table.T, heating, precision=highest),
                jnp.dot(sine_table.T, heating, precision=highest),
            ],
            1,
        )
        / total_lon,
        "lon",
        scatter_dimension=0,
        tiled=True,
    )
    my_modes = lon_index * mode_local + jnp.arange(mode_local, dtype=jnp.int32)
    my_lats = lat_index * lat_local + jnp.arange(lat_local, dtype=jnp.int32)
    table = legendre(my_modes, my_lats, total_lat, NN)
    weights = latitude_weights(my_lats, total_lat)
    partial_spec = jnp.einsum(
        "mnj,mcj->mcn", table, coefs * weights[None, None, :], precision=highest
    )
    spectrum = lax.psum(partial_spec, "lat")
    my_trunc = lax.dynamic_slice_in_dim(truncation, lon_index * mode_local, mode_local)
    degrees = jnp.arange(NN, dtype=jnp.int32)
    keep_mask = (
        (degrees[None, :] >= my_modes[:, None]) & (degrees[None, :] <= my_trunc[:, None])
    ).astype(jnp.float32)
    filtered = jnp.einsum(
        "mnj,mcn->mcj", table, spectrum * keep_mask[:, None, :], precision=highest
    )
    piece = lax.all_gather(filtered, "lon", axis=0, tiled=True)
    modes = jnp.arange(piece.shape[0], dtype=jnp.int32)
    cosine_table, sine_table = wave_table(my_lons, modes, total_lon)
    factor = jnp.where(modes == 0, 1.0, 2.0).astype(jnp.float32)[:, None]
    forcing = jnp.dot(cosine_table, factor * piece[:, 0], precision=highest) + jnp.dot(
        sine_table, factor * piece[:, 1], precision=highest
    )
    level_profile = jnp.sin(jnp.pi * (jnp.arange(levels).astype(jnp.float32) + 0.5) / levels)
    profile = jnp.tile(level_profile, columns_across)
    rate = jnp.tile(courant, columns_across)[None, None, :]
    blocks_count = 8
    block_rows = lon_local // blocks_count
    block_cost = jnp.max(counts.reshape(blocks_count, block_rows, lat_local), axis=(1, 2))

    def visit(block_index, updated):
        start = block_index * block_rows
        piece = lax.dynamic_slice_in_dim(cloud_state, start, block_rows, 1)
        force_rows = lax.dynamic_slice_in_dim(forcing, start, block_rows, 0)
        count_rows = lax.dynamic_slice_in_dim(counts, start, block_rows, 0)
        result = run_block(
            piece, force_rows, count_rows, rate, profile, levels, block_cost[block_index]
        )
        return lax.dynamic_update_slice_in_dim(updated, result, start, 1)

    updated = lax.fori_loop(0, blocks_count, visit, cloud_state)
    return updated


def solution(mesh):
    return jax.shard_map(
        shards,
        mesh=mesh,
        in_specs=(P("grp", "lon", "lat", None), P(("grp", "lon"), "lat"), P(), P()),
        out_specs=P("grp", "lon", "lat", None),
        check_vma=False,
    )
```

profile of v0, /device:TPU:8, one launch (start us, length us, event | category | flops | bytes accessed | tf_op | source)
XLA Modules:
  0.0 384.5 jit_solution(14909525809693610050)
XLA Ops:
  4.3 3.8 slice_reduce_fusion
  8.8 35.5 %all-reduce = f32[96,2,64]{2,1,0:T(2,128)S(1)} all-reduce(f32[96,2,64]{2,1,0:T(2,128)S(1)} %copy.12), channel_id=2, replica_groups=mesh['grp'=2,'lon'=8,'lat'=2] {'lon'}, use_global_device_ids=true, to_apply=%region_1.2.clone | all-reduce | flops 12288 | bytes 98304
  44.4 82.5 %while.81 = (s32[]{:T(128)}, f32[12,64]{1,0:T(8,128)S(1)}, f32[12,64]{1,0:T(8,128)S(1)}, f32[12]{0:T(128)S(1)}, f32[12,8,12,64]{3,2,1,0:T(8,128)S(1)}, /*index=5...) while((s32[]{:T(128)}, f32[12,64]{1,0:T(8,128)S(1)}, ...), condition=%wide.region_4.5_spmd.clone.clone.clone, body=%wide.region_3.4_spmd.clone.clone.clone.sunk | while | flops 108922 | bytes 421596 | solution.py:35
  127.6 3.3 psum.7
  131.6 30.6 %all_gather.3 = f32[96,2,64]{2,1,0:T(2,128)S(1)} all-gather(f32[12,2,64]{2,1,0:T(2,128)S(1)} %fusion.42), channel_id=1, replica_groups=mesh['grp'=2,'lon'=8,'lat'=2] {'lon'}, dimensions={0}, use_global_device_ids=true | all-gather | bytes 55296 | tf_op jit(solution)/shard_map/all_gather | solution.py:124
  162.8 12.0 %copy.50 = f32[2,32,64,1024]{3,2,1,0:T(8,128)} copy(f32[2,32,64,1024]{3,2,1,0:T(8,128)} %param.10) | data formatting | bytes 33554432
  174.8 209.7 %while.80 = (s32[]{:T(128)}, f32[2,32,64,1024]{3,2,1,0:T(8,128)}, f32[2,32,64,1024]{3,2,1,0:T(8,128)}, s32[8]{0:T(128)S(1)}, f32[32,64]{1,0:T(8,128)S(1)}, /*ind...) while((s32[]{:T(128)}, f32[2,32,64,1024]{3,2,1,0:T(8,128)}, ...), condition=%wide.region_11.12_spmd.clone, body=%wide.region_8.11_spmd.clone.sunk | while | flops 6817033 | bytes 18993312 | solution.py:148
  176.2 1.7 dynamic-slice_bitcast_fusion.3
  177.9 21.7 %while.82 = (s32[]{:T(128)}, f32[4,64,1024]{2,1,0:T(8,128)S(1)}, f32[4,64,1024]{2,1,0:T(8,128)S(1)}, s32[]{:T(128)}, s32[4,64]{1,0:T(4,128)S(1)}, /*index=5*/f32...) while((s32[]{:T(128)}, f32[4,64,1024]{2,1,0:T(8,128)S(1)}, ...), condition=%wide.region_10.10_spmd, body=%wide.region_9.9_spmd.sunk | while | flops 6292738 | bytes 10583657 | solution.py:73
  179.1 1.4 subtract_select_fusion.2
  181.7 1.4 subtract_select_fusion.2
  184.3 1.4 subtract_select_fusion.2
  192.2 1.4 subtract_select_fusion.2
  194.9 1.4 subtract_select_fusion.2
  197.5 1.4 subtract_select_fusion.2
  199.6 1.5 maximum_dynamic-update-slice_fusion.2
  202.4 1.7 dynamic-slice_bitcast_fusion.3
  204.1 21.7 %while.82 = (s32[]{:T(128)}, f32[4,64,1024]{2,1,0:T(8,128)S(1)}, f32[4,64,1024]{2,1,0:T(8,128)S(1)}, s32[]{:T(128)}, s32[4,64]{1,0:T(4,128)S(1)}, /*index=5*/f32...) while((s32[]{:T(128)}, f32[4,64,1024]{2,1,0:T(8,128)S(1)}, ...), condition=%wide.region_10.10_spmd, body=%wide.region_9.9_spmd.sunk | while | flops 6292738 | bytes 10583657 | solution.py:73
  205.3 1.4 subtract_select_fusion.2
  207.9 1.4 subtract_select_fusion.2
  210.5 1.4 subtract_select_fusion.2
  215.8 1.4 subtract_select_fusion.2
  218.4 1.4 subtract_select_fusion.2
  221.1 1.4 subtract_select_fusion.2
  223.7 1.4 subtract_select_fusion.2
  225.8 1.5 maximum_dynamic-update-slice_fusion.2
  228.6 1.7 dynamic-slice_bitcast_fusion.3
  230.3 21.7 %while.82 = (s32[]{:T(128)}, f32[4,64,1024]{2,1,0:T(8,128)S(1)}, f32[4,64,1024]{2,1,0:T(8,128)S(1)}, s32[]{:T(128)}, s32[4,64]{1,0:T(4,128)S(1)}, /*index=5*/f32...) while((s32[]{:T(128)}, f32[4,64,1024]{2,1,0:T(8,128)S(1)}, ...), condition=%wide.region_10.10_spmd, body=%wide.region_9.9_spmd.sunk | while | flops 6292738 | bytes 10583657 | solution.py:73
  231.5 1.4 subtract_select_fusion.2
  234.1 1.4 subtract_select_fusion.2
  242.0 1.4 subtract_select_fusion.2
  244.7 1.4 subtract_select_fusion.2
  247.3 1.4 subtract_select_fusion.2
  252.0 1.5 maximum_dynamic-update-slice_fusion.2
  254.8 1.7 dynamic-slice_bitcast_fusion.3
  256.5 21.7 %while.82 = (s32[]{:T(128)}, f32[4,64,1024]{2,1,0:T(8,128)S(1)}, f32[4,64,1024]{2,1,0:T(8,128)S(1)}, s32[]{:T(128)}, s32[4,64]{1,0:T(4,128)S(1)}, /*index=5*/f32...) while((s32[]{:T(128)}, f32[4,64,1024]{2,1,0:T(8,128)S(1)}, ...), condition=%wide.region_10.10_spmd, body=%wide.region_9.9_spmd.sunk | while | flops 6292738 | bytes 10583657 | solution.py:73
  257.7 1.4 subtract_select_fusion.2
  260.3 1.4 subtract_select_fusion.2
  265.6 1.4 subtract_select_fusion.2
  268.2 1.4 subtract_select_fusion.2
  270.9 1.4 subtract_select_fusion.2
  273.5 1.4 subtract_select_fusion.2
  278.2 1.5 maximum_dynamic-update-slice_fusion.2
  281.0 1.7 dynamic-slice_bitcast_fusion.3
  282.7 21.7 %while.82 = (s32[]{:T(128)}, f32[4,64,1024]{2,1,0:T(8,128)S(1)}, f32[4,64,1024]{2,1,0:T(8,128)S(1)}, s32[]{:T(128)}, s32[4,64]{1,0:T(4,128)S(1)}, /*index=5*/f32...) while((s32[]{:T(128)}, f32[4,64,1024]{2,1,0:T(8,128)S(1)}, ...), condition=%wide.region_10.10_spmd, body=%wide.region_9.9_spmd.sunk | while | flops 6292738 | bytes 10583657 | solution.py:73
  283.9 1.4 subtract_select_fusion.2
  291.8 1.4 subtract_select_fusion.2
  294.5 1.4 subtract_select_fusion.2
  297.1 1.4 subtract_select_fusion.2
  302.4 1.4 subtract_select_fusion.2
  304.4 1.5 maximum_dynamic-update-slice_fusion.2
  307.3 1.7 dynamic-slice_bitcast_fusion.3
  308.9 21.7 %while.82 = (s32[]{:T(128)}, f32[4,64,1024]{2,1,0:T(8,128)S(1)}, f32[4,64,1024]{2,1,0:T(8,128)S(1)}, s32[]{:T(128)}, s32[4,64]{1,0:T(4,128)S(1)}, /*index=5*/f32...) while((s32[]{:T(128)}, f32[4,64,1024]{2,1,0:T(8,128)S(1)}, ...), condition=%wide.region_10.10_spmd, body=%wide.region_9.9_spmd.sunk | while | flops 6292738 | bytes 10583657 | solution.py:73
  310.1 1.4 subtract_select_fusion.2
  315.4 1.4 subtract_select_fusion.2
  318.0 1.4 subtract_select_fusion.2
  320.7 1.4 subtract_select_fusion.2
  330.6 1.5 maximum_dynamic-update-slice_fusion.2
  333.5 1.7 dynamic-slice_bitcast_fusion.3
  335.2 21.7 %while.82 = (s32[]{:T(128)}, f32[4,64,1024]{2,1,0:T(8,128)S(1)}, f32[4,64,1024]{2,1,0:T(8,128)S(1)}, s32[]{:T(128)}, s32[4,64]{1,0:T(4,128)S(1)}, /*index=5*/f32...) while((s32[]{:T(128)}, f32[4,64,1024]{2,1,0:T(8,128)S(1)}, ...), condition=%wide.region_10.10_spmd, body=%wide.region_9.9_spmd.sunk | while | flops 6292738 | bytes 10583657 | solution.py:73
  356.9 1.5 maximum_dynamic-update-slice_fusion.2
  359.7 1.7 dynamic-slice_bitcast_fusion.3
  361.4 21.7 %while.82 = (s32[]{:T(128)}, f32[4,64,1024]{2,1,0:T(8,128)S(1)}, f32[4,64,1024]{2,1,0:T(8,128)S(1)}, s32[]{:T(128)}, s32[4,64]{1,0:T(4,128)S(1)}, /*index=5*/f32...) while((s32[]{:T(128)}, f32[4,64,1024]{2,1,0:T(8,128)S(1)}, ...), condition=%wide.region_10.10_spmd, body=%wide.region_9.9_spmd.sunk | while | flops 6292738 | bytes 10583657 | solution.py:73
  383.1 1.5 maximum_dynamic-update-slice_fusion.2
  (909 shorter events, 115.2 us)
Async XLA Ops:
  162.8 12.0 %copy-start = (f32[32]{0:T(128)S(1)}, f32[32]{0:T(128)}, u32[]{:S(2)}) copy-start(f32[32]{0:T(128)} %param.12) | copy-start | bytes 388
where the time goes:
time: 387 us; the launch traced here: 385 us
  other arithmetic  131 us (34%)
  loops' own time  111 us (29%)
  local copies, waits for them, and re-layouts  70.2 us (18%)
  blocking collectives  69.3 us (18%)
    select_n x64, other arithmetic, substep(): jnp.where(active, moved_moist - condensed, moist)  91.4 us
    another operation x1, loops' own time, legendre(): lax.scan(legendre_advance, initial, jnp.arange(degrees, dtype=jnp.int32),...  62.2 us
    another operation x8, loops' own time, run_block(): lax.while_loop(unfinished, run_advance, (jnp.int32(0), block_state[0], bl...  48.8 us
    unnamed x1, blocking collectives  35.5 us
    all_gather x1, blocking collectives, shards(): piece = lax.all_gather(filtered, 'lon', axis=0, tiled=True)  30.6 us
    squeeze x8, local copies, waits for them, and re-layouts, run_block(): block_state[1]  13.4 us
    unnamed x4, local copies, waits for them, and re-layouts  13.3 us
    dynamic_update_slice x8, other arithmetic, visit(): return lax.dynamic_update_slice_in_dim(updated, result, start, 1)  11.7 us

commit v1 on v0

--- a/solution.py
+++ b/solution.py
@@ -5,6 +5,18 @@
 
 NN = 96
 couple_gain = 8.0
+
+
+def collect(shard, axis, dim):
+    ways, here, turn = (lax.axis_size(axis), lax.axis_index(axis), shard.shape[dim])
+    line, have = (shard, 1)
+    while have < ways:
+        line = jnp.concatenate(
+            [line, lax.ppermute(line, axis, [(d, (d - have) % ways) for d in range(ways)])],
+            axis=dim,
+        )
+        have = 2 * have
+    return jnp.roll(line, here * turn, axis=dim)
 
 
 def legendre(orders, lat_rows, lat_total, degrees):
@@ -121,7 +133,7 @@
     filtered = jnp.einsum(
         "mnj,mcn->mcj", table, spectrum * keep_mask[:, None, :], precision=highest
     )
-    piece = lax.all_gather(filtered, "lon", axis=0, tiled=True)
+    piece = collect(filtered, "lon", 0)
     modes = jnp.arange(piece.shape[0], dtype=jnp.int32)
     cosine_table, sine_table = wave_table(my_lons, modes, total_lon)
     factor = jnp.where(modes == 0, 1.0, 2.0).astype(jnp.float32)[:, None]

time: 387 us -> 365 us (0.943)
  blocking collectives: 69.3 us -> 38.8 us
  starting transfers between devices: 0 us -> 6.55 us
  loops' own time: 111 us -> 116 us
  local copies, waits for them, and re-layouts: 70.2 us -> 65.4 us
    all_gather x1 -> x0, blocking collectives: 30.6 us -> none  [shards(): piece = lax.all_gather(filtered, 'lon', axis=0, tiled=True)]
    ppermute x0 -> x3, starting transfers between devices: none -> 6.55 us  [collect(): lax.ppermute(line, axis, [(d, (d - have) % ways) for d in range(ways)])]
    dynamic_slice x8, local copies, waits for them, and re-layouts: 5.53 us -> 0.05 us  [visit(): count_rows = lax.dynamic_slice_in_dim(counts, start, block_rows, 0)]
    another operation x8, loops' own time: 48.8 us -> 53.4 us  [run_block(): lax.while_loop(unfinished, run_advance, (jnp.int32(0), block_state[0], bl...]
    unnamed x4 -> x12, local copies, waits for them, and re-layouts: 13.3 us -> 13.3 us
  transfers between devices with their start and end apart: 0 -> 3, of which waited for: 0 -> 2; matrix products, arithmetic and copies ran while one was open for 0% -> 3% of each run, Pallas kernels for 0% -> 0%
where the time goes in v1:
time: 365 us; the launch traced here: 363 us
  other arithmetic  130 us (36%)
  loops' own time  116 us (32%)
  local copies, waits for them, and re-layouts  65.4 us (18%)
  blocking collectives  38.8 us (11%)
  starting transfers between devices  6.55 us (2%)
    select_n x64, other arithmetic, substep(): jnp.where(active, moved_moist - condensed, moist)  91.4 us
    another operation x1, loops' own time, legendre(): lax.scan(legendre_advance, initial, jnp.arange(degrees, dtype=jnp.int32),...  62.1 us
    another operation x8, loops' own time, run_block(): lax.while_loop(unfinished, run_advance, (jnp.int32(0), block_state[0], bl...  53.4 us
    unnamed x1, blocking collectives  35.5 us
    squeeze x8, local copies, waits for them, and re-layouts, run_block(): block_state[1]  13.4 us
    unnamed x12, local copies, waits for them, and re-layouts  13.3 us
    dynamic_update_slice x8, other arithmetic, visit(): return lax.dynamic_update_slice_in_dim(updated, result, start, 1)  11.7 us
    add x64, other arithmetic, substep(): heated = theta + couple_gain * profile[None, None, :] * force[:, :, None]  9.97 us
  transfers between devices with their start and end apart: 3, of which 2 were waited for; matrix products, arithmetic and copies ran while one was open for 3% of the time, Pallas kernels for 0%

profile of v1, /device:TPU:8, one launch (start us, length us, event | category | flops | bytes accessed | tf_op | source)
XLA Modules:
  0.0 363.1 jit_solution(8892459899098874213)
XLA Ops:
  0.2 3.8 %slice_reduce_fusion = f32[32,64]{1,0:T(8,128)S(1)} fusion(f32[2,32,64,1024]{3,2,1,0:T(8,128)} %param.10), kind=kLoop, calls=%fused_computation.96 | loop fusion | flops 2095104 | bytes 8396800 | tf_op jit(solution)/shard_map/reduce_sum | solution.py:103
  5.0 35.5 %all-reduce = f32[96,2,64]{2,1,0:T(2,128)S(1)} all-reduce(f32[96,2,64]{2,1,0:T(2,128)S(1)} %copy.12), channel_id=2, replica_groups=mesh['grp'=2,'lon'=8,'lat'=2] {'lon'}, use_global_device_ids=true, to_apply=%region_1.2.clone | all-reduce | flops 12288 | bytes 98304
  40.5 82.5 %while.81 = (s32[]{:T(128)}, f32[12,64]{1,0:T(8,128)S(1)}, f32[12,64]{1,0:T(8,128)S(1)}, f32[12]{0:T(128)S(1)}, f32[12,8,12,64]{3,2,1,0:T(8,128)S(1)}, /*index=5...) while((s32[]{:T(128)}, f32[12,64]{1,0:T(8,128)S(1)}, ...), condition=%wide.region_4.5_spmd.clone.clone.clone, body=%wide.region_3.4_spmd.clone.clone.clone.sunk | while | flops 108922 | bytes 421596 | solution.py:47
  125.6 3.3 psum.7
  130.5 12.0 %copy.57 = f32[2,32,64,1024]{3,2,1,0:T(8,128)} copy(f32[2,32,64,1024]{3,2,1,0:T(8,128)} %param.10) | data formatting | bytes 33554432
  142.9 3.3 collective-permute-start.1
  146.2 1.5 collective-permute-done.1
  147.7 3.2 collective-permute-start.2
  151.0 2.1 collective-permute-done.2
  153.8 209.4 %while.80 = (s32[]{:T(128)}, f32[2,32,64,1024]{3,2,1,0:T(8,128)}, f32[2,32,64,1024]{3,2,1,0:T(8,128)}, s32[8]{0:T(128)S(1)}, f32[32,64]{1,0:T(8,128)S(1)}, /*ind...) while((s32[]{:T(128)}, f32[2,32,64,1024]{3,2,1,0:T(8,128)}, ...), condition=%wide.region_11.12_spmd.clone, body=%wide.region_8.11_spmd.clone.sunk | while | flops 6817033 | bytes 18993312 | solution.py:160
  154.6 1.7 dynamic-slice_bitcast_fusion.3
  156.3 22.3 %while.82 = (s32[]{:T(128)}, f32[4,64,1024]{2,1,0:T(8,128)S(1)}, f32[4,64,1024]{2,1,0:T(8,128)S(1)}, s32[]{:T(128)}, s32[4,64]{1,0:T(4,128)S(1)}, /*index=5*/f32...) while((s32[]{:T(128)}, f32[4,64,1024]{2,1,0:T(8,128)S(1)}, ...), condition=%wide.region_10.10_spmd, body=%wide.region_9.9_spmd.sunk | while | flops 6292738 | bytes 10583657 | solution.py:85
  165.6 1.4 subtract_select_fusion.2
  168.3 1.4 subtract_select_fusion.2
  171.0 1.4 subtract_select_fusion.2
  173.7 1.4 subtract_select_fusion.2
  176.4 1.4 subtract_select_fusion.2
  178.5 1.5 maximum_dynamic-update-slice_fusion.2
  180.7 1.7 dynamic-slice_bitcast_fusion.3
  182.4 22.3 %while.82 = (s32[]{:T(128)}, f32[4,64,1024]{2,1,0:T(8,128)S(1)}, f32[4,64,1024]{2,1,0:T(8,128)S(1)}, s32[]{:T(128)}, s32[4,64]{1,0:T(4,128)S(1)}, /*index=5*/f32...) while((s32[]{:T(128)}, f32[4,64,1024]{2,1,0:T(8,128)S(1)}, ...), condition=%wide.region_10.10_spmd, body=%wide.region_9.9_spmd.sunk | while | flops 6292738 | bytes 10583657 | solution.py:85
  183.7 1.4 subtract_select_fusion.2
  186.4 1.4 subtract_select_fusion.2
  197.2 1.4 subtract_select_fusion.2
  199.9 1.4 subtract_select_fusion.2
  202.6 1.4 subtract_select_fusion.2
  204.7 1.5 maximum_dynamic-update-slice_fusion.2
  206.9 1.7 dynamic-slice_bitcast_fusion.3
  208.6 22.3 %while.82 = (s32[]{:T(128)}, f32[4,64,1024]{2,1,0:T(8,128)S(1)}, f32[4,64,1024]{2,1,0:T(8,128)S(1)}, s32[]{:T(128)}, s32[4,64]{1,0:T(4,128)S(1)}, /*index=5*/f32...) while((s32[]{:T(128)}, f32[4,64,1024]{2,1,0:T(8,128)S(1)}, ...), condition=%wide.region_10.10_spmd, body=%wide.region_9.9_spmd.sunk | while | flops 6292738 | bytes 10583657 | solution.py:85
  209.9 1.4 subtract_select_fusion.2
  212.5 1.4 subtract_select_fusion.2
  215.2 1.4 subtract_select_fusion.2
  217.9 1.4 subtract_select_fusion.2
  228.7 1.4 subtract_select_fusion.2
  230.9 1.5 maximum_dynamic-update-slice_fusion.2
  233.1 1.7 dynamic-slice_bitcast_fusion.3
  234.8 22.3 %while.82 = (s32[]{:T(128)}, f32[4,64,1024]{2,1,0:T(8,128)S(1)}, f32[4,64,1024]{2,1,0:T(8,128)S(1)}, s32[]{:T(128)}, s32[4,64]{1,0:T(4,128)S(1)}, /*index=5*/f32...) while((s32[]{:T(128)}, f32[4,64,1024]{2,1,0:T(8,128)S(1)}, ...), condition=%wide.region_10.10_spmd, body=%wide.region_9.9_spmd.sunk | while | flops 6292738 | bytes 10583657 | solution.py:85
  236.0 1.4 subtract_select_fusion.2
  238.7 1.4 subtract_select_fusion.2
  241.4 1.4 subtract_select_fusion.2
  244.1 1.4 subtract_select_fusion.2
  246.8 1.4 subtract_select_fusion.2
  249.5 1.4 subtract_select_fusion.2
  257.0 1.5 maximum_dynamic-update-slice_fusion.2
  259.2 1.7 dynamic-slice_bitcast_fusion.3
  260.9 22.3 %while.82 = (s32[]{:T(128)}, f32[4,64,1024]{2,1,0:T(8,128)S(1)}, f32[4,64,1024]{2,1,0:T(8,128)S(1)}, s32[]{:T(128)}, s32[4,64]{1,0:T(4,128)S(1)}, /*index=5*/f32...) while((s32[]{:T(128)}, f32[4,64,1024]{2,1,0:T(8,128)S(1)}, ...), condition=%wide.region_10.10_spmd, body=%wide.region_9.9_spmd.sunk | while | flops 6292738 | bytes 10583657 | solution.py:85
  264.9 1.4 subtract_select_fusion.2
  267.6 1.4 subtract_select_fusion.2
  270.3 1.4 subtract_select_fusion.2
  273.0 1.4 subtract_select_fusion.2
  275.7 1.4 subtract_select_fusion.2
  278.4 1.4 subtract_select_fusion.2
  281.1 1.4 subtract_select_fusion.2
  283.2 1.5 maximum_dynamic-update-slice_fusion.2
  285.4 1.7 dynamic-slice_bitcast_fusion.3
  287.1 22.3 %while.82 = (s32[]{:T(128)}, f32[4,64,1024]{2,1,0:T(8,128)S(1)}, f32[4,64,1024]{2,1,0:T(8,128)S(1)}, s32[]{:T(128)}, s32[4,64]{1,0:T(4,128)S(1)}, /*index=5*/f32...) while((s32[]{:T(128)}, f32[4,64,1024]{2,1,0:T(8,128)S(1)}, ...), condition=%wide.region_10.10_spmd, body=%wide.region_9.9_spmd.sunk | while | flops 6292738 | bytes 10583657 | solution.py:85
  288.4 1.4 subtract_select_fusion.2
  296.4 1.4 subtract_select_fusion.2
  309.4 1.5 maximum_dynamic-update-slice_fusion.2
  311.6 1.7 dynamic-slice_bitcast_fusion.3
  313.3 22.3 %while.82 = (s32[]{:T(128)}, f32[4,64,1024]{2,1,0:T(8,128)S(1)}, f32[4,64,1024]{2,1,0:T(8,128)S(1)}, s32[]{:T(128)}, s32[4,64]{1,0:T(4,128)S(1)}, /*index=5*/f32...) while((s32[]{:T(128)}, f32[4,64,1024]{2,1,0:T(8,128)S(1)}, ...), condition=%wide.region_10.10_spmd, body=%wide.region_9.9_spmd.sunk | while | flops 6292738 | bytes 10583657 | solution.py:85
  335.5 1.5 maximum_dynamic-update-slice_fusion.2
  337.7 1.7 dynamic-slice_bitcast_fusion.3
  339.4 22.3 %while.82 = (s32[]{:T(128)}, f32[4,64,1024]{2,1,0:T(8,128)S(1)}, f32[4,64,1024]{2,1,0:T(8,128)S(1)}, s32[]{:T(128)}, s32[4,64]{1,0:T(4,128)S(1)}, /*index=5*/f32...) while((s32[]{:T(128)}, f32[4,64,1024]{2,1,0:T(8,128)S(1)}, ...), condition=%wide.region_10.10_spmd, body=%wide.region_9.9_spmd.sunk | while | flops 6292738 | bytes 10583657 | solution.py:85
  361.7 1.5 maximum_dynamic-update-slice_fusion.2
  (925 shorter events, 114.0 us)
Async XLA Ops:
  130.4 12.4 %collective-permute-start = (f32[12,2,64]{2,1,0:T(2,128)S(1)}, f32[12,2,64]{2,1,0:T(2,128)S(1)}, u32[]{:S(2)}, u32[]{:S(2)}) collective-permute-start(f32[12,2,64]{2,1,0:T(2,128)S(1)} %get-tuple-element.757), channel_id=1, source_target_pairs={{0,14},{2,0},{4,2},{6,4},{8,6},{10,8},{12,10},{14,12},{1,15},{3,1}... | collective-permute-start | bytes 18440 | tf_op jit(solution)/shard_map/ppermute | solution.py:15
  130.5 12.0 %copy-start = (s32[32,64]{1,0:T(8,128)S(1)}, s32[32,64]{1,0:T(8,128)}, u32[]{:S(2)}) copy-start(s32[32,64]{1,0:T(8,128)} %param.11) | copy-start | bytes 24580
  130.5 23.3 %copy-start.1 = (f32[32]{0:T(128)S(1)}, f32[32]{0:T(128)}, u32[]{:S(2)}) copy-start(f32[32]{0:T(128)} %param.12) | copy-start | bytes 388
  142.9 4.8 %collective-permute-start.1 = (f32[24,2,64]{2,1,0:T(2,128)S(1)}, f32[24,2,64]{2,1,0:T(2,128)S(1)}, u32[]{:S(2)}, u32[]{:S(2)}) collective-permute-start(f32[24,2,64]{2,1,0:T(2,128)S(1)} %pad_maximum_fusion.1), channel_id=1, source_target_pairs={{0,12},{2,14},{4,0},{6,2},{8,4},{10,6},{12,8},{14,10},{1,13},{3,15... | collective-permute-start | bytes 36872 | tf_op jit(solution)/shard_map/ppermute | solution.py:15
  147.7 5.3 %collective-permute-start.2 = (f32[48,2,64]{2,1,0:T(2,128)S(1)}, f32[48,2,64]{2,1,0:T(2,128)S(1)}, u32[]{:S(2)}, u32[]{:S(2)}) collective-permute-start(f32[48,2,64]{2,1,0:T(2,128)S(1)} %pad_maximum_fusion), channel_id=1, source_target_pairs={{0,8},{2,10},{4,12},{6,14},{8,0},{10,2},{12,4},{14,6},{1,9},{3,11}... | collective-permute-start | bytes 73736 | tf_op jit(solution)/shard_map/ppermute | solution.py:15
